TPU v7x, 128 devices: a whole 4x4x4 slice. The times are simulated.
128 devices in a mesh: row: 16 (over z, x_hi, core), col: 8 (over x_lo, y).
Axes of the slice: x: 4 (x_hi: 2, x_lo: 2; x = x_hi * 2 + x_lo), y: 4, z: 4, core: 2. Of those that a mesh axis runs over, the one named last changes fastest.
Arguments:
- stored: bfloat16 [1024, 51200], P(('row', 'col')), may hold values from -24 to 24
- integrals: bfloat16 [51200, 25600], P('row', 'col'), may hold values from -0.02734375 to 0.02734375
- layout: int32 [1024], replicated, may hold values from 0 to 1023, each once
- partner: int32 [1024], replicated, may hold values from 0 to 1023, as said below
Outputs:
- residual_out: bfloat16 [1024, 25600], P('row', 'col')
Inputs may be any that keep to these rules, and one draw needn't show every extreme that they name: partner is an involution without fixed points: partner[p] != p and partner[partner[p]] = p. `layout`: each slab pair stands in exactly one stored row.
All inputs are finite; a program needn't handle non-finite values.
Results may differ from a plain program's by a relative error of at most 0.001.
Values may be sent and summed in bfloat16 or wider, within the bound.
A program may use at most 128 MiB of HBM per device.

v0:
```python
import jax
import jax.numpy as jnp
from jax import lax
from jax.sharding import Mesh, PartitionSpec as P

ROW_AXES = ("z", "xh", "core")
COL_AXES = ("xl", "y")


def per_device(stored, integrals, layout, partner):
    local_rows = stored.shape[0]
    n_z = lax.axis_size("z")
    n_xh = lax.axis_size("xh")
    n_core = lax.axis_size("core")
    n_row = n_z * n_xh * n_core
    n_col = lax.axis_size(COL_AXES)
    total = local_rows * n_row * n_col
    block = total // n_row
    regrouped = lax.all_to_all(stored, ROW_AXES, split_axis=1, concat_axis=0, tiled=True)
    gathered = lax.all_gather(regrouped, COL_AXES, axis=0, tiled=True)
    s = jnp.arange(total, dtype=jnp.int32)
    s_row = s // (local_rows * n_col)
    s_col = s // local_rows % n_col
    s_off = s % local_rows
    pos_of_stored = s_col * (n_row * local_rows) + s_row * local_rows + s_off
    inv = jnp.zeros((total,), jnp.int32).at[layout].set(s)
    i = jnp.arange(total, dtype=jnp.int32)
    g = i // block
    xh = g % n_xh
    core = g // n_xh % n_core
    z = g // (n_xh * n_core)
    p_of_i = ((z * n_xh + xh) * n_core + core) * block + i % block
    q = partner[p_of_i]
    q_g = q // block
    q_core = q_g % n_core
    q_xh = q_g // n_core % n_xh
    q_z = q_g // (n_core * n_xh)
    partner_i = ((q_z * n_core + q_core) * n_xh + q_xh) * block + q % block
    amps = gathered[pos_of_stored[inv[p_of_i]]]
    ladder = jnp.dot(amps, integrals, preferred_element_type=jnp.float32)
    difference = ladder - ladder[partner_i]
    part = lax.psum_scatter(difference, ("z", "core"), scatter_dimension=0, tiled=True)
    part = lax.psum_scatter(part, "xh", scatter_dimension=0, tiled=True)
    return part.astype(jnp.bfloat16)


def solution(mesh):
    n_row, n_col = mesh.devices.shape
    fine = Mesh(mesh.devices.reshape(4, n_row // 8, 2, 2, n_col // 2), ROW_AXES + COL_AXES)
    return jax.shard_map(
        per_device,
        mesh=fine,
        in_specs=(P(ROW_AXES + COL_AXES, None), P(ROW_AXES, COL_AXES), P(), P()),
        out_specs=P(ROW_AXES, COL_AXES),
        check_vma=False,
    )
```

profile of v0, /device:TPU:1, one launch (start us, length us, event | category | flops | bytes accessed | tf_op | source)
XLA Modules:
  0.0 296.2 jit_solution(10515165706835330987)
XLA Ops:
  6.5 0.0 copy-start
  6.5 0.0 all-gather.2.cloned.1.call-start
  6.5 24.0 %all_to_all.19 = bf16[8,16,3200]{2,0,1:T(8,128)(2,1)} all-to-all(bf16[8,16,3200]{2,0,1:T(8,128)(2,1)} %bitcast.15), channel_id=1, replica_groups=mesh['z'=4,'xh'=2,'core'=2,'xl'=2,'y'=4] {'z','xh','core'}, dimensions={1} | all-to-all | bytes 1638400 | tf_op jit(solution)/shard_map/all_to_all | solution.py:19
  30.6 0.0 all-gather.2.cloned.1.call-update
  30.6 0.0 reduce-scatter.3.cloned.1.call-start
  30.7 0.0 copy-done
  30.7 4.5 %gather_fusion.3 = s32[1024]{0:T(1024)S(1)} fusion(s32[1024]{0:T(1024)S(1)} %copy-done, s32[1024]{0:T(1024)S(1)} %broadcast_clamp_fusion.1), kind=kCustom, calls=%fused_computation.3 | custom fusion | bytes 12288 | tf_op jit(solution)/shard_map/gather | solution.py:33
  35.2 0.7 compare_select_fusion.8
  35.9 4.3 %scatter_custom_fusion = s32[1024]{0:T(1024)S(1)} fusion(s32[1024]{0:T(1024)S(1)} %compare_select_fusion.8, s32[1024]{0:T(1024)S(1)} %iota.13, s32[]{:T(128)} %constant.129.clone.1), kind=kCustom, calls=%fused_computation.79 | custom fusion | bytes 4100 | tf_op jit(solution)/shard_map/scatter | solution.py:26
  40.3 4.5 %gather_fusion = s32[1024]{0:T(1024)S(1)} fusion(s32[1024]{0:T(1024)S(1)} %scatter_custom_fusion, s32[1024]{0:T(1024)S(1)} %broadcast_clamp_fusion.1), kind=kCustom, calls=%fused_computation | custom fusion | bytes 12288 | tf_op jit(solution)/shard_map/gather | solution.py:39
  44.8 4.5 %gather_fusion.1 = s32[1024]{0:T(1024)S(1)} fusion(s32[1024]{0:T(1024)S(1)} %get-tuple-element.5, s32[1024]{0:T(1024)S(1)} %get-tuple-element.6), kind=kCustom, calls=%fused_computation.1 | custom fusion | bytes 12288 | tf_op jit(solution)/shard_map/gather | solution.py:39
  49.4 0.1 compare_select_fusion
  49.5 53.2 %all-gather.2.cloned.1.call-done = bf16[1024,3200]{1,0:T(8,128)(2,1)} async-done(((bf16[128,3200]{1,0:T(8,128)(2,1)}), bf16[1024,3200]{1,0:T(8,128)(2,1)}) %all-gather.2.cloned.1.call-update) | async-done | bytes 6553616 | tf_op jit(solution)/shard_map/all_gather | solution.py:20
  102.7 16.3 %gather_fusion.2 = bf16[1024,3200]{1,0:T(8,128)(2,1)} fusion(bf16[1024,3200]{1,0:T(8,128)(2,1)} %all-gather.2.cloned.1.call-done, s32[1024]{0:T(1024)S(1)} %broadcast_clamp_fusion.3), kind=kCustom, calls=%fused_computation.2 | custom fusion | bytes 13111296 | tf_op jit(solution)/shard_map/gather | solution.py:39
  119.0 30.5 %fusion.24 = f32[1024,3200]{1,0:T(8,128)} fusion(bf16[1024,3200]{1,0:T(8,128)(2,1)} %gather_fusion.2, bf16[3200,3200]{1,0:T(8,128)(2,1)} %param.5), kind=kOutput, calls=%fused_computation.81 | convolution fusion | flops 20971520000 | bytes 40140800 | tf_op jit(solution)/shard_map/dot_general | solution.py:40
  149.5 17.1 %gather_fusion.4 = f32[1024,3200]{1,0:T(8,128)} fusion(f32[1024,3200]{1,0:T(8,128)} %fusion.24, s32[1024]{0:T(1024)S(1)} %broadcast_clamp_fusion), kind=kCustom, calls=%fused_computation.4 | custom fusion | bytes 26218496 | tf_op jit(solution)/shard_map/gather | solution.py:41
  166.7 0.0 copy-start.1
  166.7 14.4 %sub.51 = f32[1024,3200]{1,0:T(8,128)} subtract(f32[1024,3200]{1,0:T(8,128)} %fusion.24, f32[1024,3200]{1,0:T(8,128)} %gather_fusion.4) | non-fusion elementwise | flops 3276800 | bytes 39321600 | tf_op jit(solution)/shard_map/sub | solution.py:41
  181.0 0.0 reduce-scatter.3.cloned.1.call-update
  181.1 0.0 reduce-scatter.5.cloned.1.call-start
  181.1 73.3 %reduce-scatter.3.cloned.1.call-done = f32[128,3200]{1,0:T(8,128)} async-done(((f32[1024,3200]{1,0:T(8,128)}), f32[128,3200]{1,0:T(8,128)}) %reduce-scatter.3.cloned.1.call-update) | async-done | bytes 1638416 | tf_op jit(solution)/shard_map/reduce_scatter | solution.py:42
  254.4 0.0 reduce-scatter.5.cloned.1.call-update
  254.4 33.4 %reduce-scatter.5.cloned.1.call-done = f32[64,3200]{1,0:T(8,128)} async-done(((f32[128,3200]{1,0:T(8,128)}), f32[64,3200]{1,0:T(8,128)}) %reduce-scatter.5.cloned.1.call-update) | async-done | bytes 819216 | tf_op jit(solution)/shard_map/reduce_scatter | solution.py:43
  287.8 1.9 convert_element_type.3
  289.7 0.0 copy-done.1
  (8 shorter events, 0.1 us)
Async XLA Ops:
  6.5 24.2 %copy-start = (s32[1024]{0:T(1024)S(1)}, s32[1024]{0:T(1024)}, u32[]{:S(2)}) copy-start(s32[1024]{0:T(1024)} %param.7) | copy-start | bytes 12292
  6.5 96.2 %all-gather.2.cloned.1.call-start = ((), (), s32[]{:S(2)}) async-start(), calls=%async_computation.3 | async-start | bytes 7372800 | tf_op jit(solution)/shard_map/all_gather | solution.py:20
  30.6 223.8 %reduce-scatter.3.cloned.1.call-start = ((), (), s32[]{:S(2)}) async-start(), calls=%async_computation.4 | async-start | bytes 14745600 | tf_op jit(solution)/shard_map/reduce_scatter | solution.py:42
  166.7 123.1 %copy-start.1 = (s32[1024]{0:T(1024)S(1)}, s32[1024]{0:T(1024)}, u32[]{:S(2)}) copy-start(s32[1024]{0:T(1024)} %param.7) | copy-start | bytes 12292
  181.1 106.7 %reduce-scatter.5.cloned.1.call-start = ((), (), s32[]{:S(2)}) async-start(), calls=%async_computation.5 | async-start | bytes 2457600 | tf_op jit(solution)/shard_map/reduce_scatter | solution.py:43
Sparse Core Ops, SparseCore 0:
  30.7 71.9 all-gather.1
  181.2 73.1 reduce-scatter.2
  256.7 30.9 reduce-scatter.4
where the time goes:
time: 297 us; the launch traced here: 296 us
  waiting for transfers between devices  160 us (54%)
  local copies, waits for them, and re-layouts  51.3 us (17%)
  matrix products  30.5 us (10%)
  blocking collectives  24 us (8%)
  other arithmetic  17.2 us (6%)
  between operations  13.2 us (4%)
    reduce_scatter x1, waiting for transfers between devices, per_device(): lax.psum_scatter(difference, ('z', 'core'), scatter_dimension=0, tiled=True)  73.3 us
    all_gather x1, waiting for transfers between devices, per_device(): gathered = lax.all_gather(regrouped, COL_AXES, axis=0, tiled=True)  53.2 us
    reduce_scatter x1, waiting for transfers between devices, per_device(): part = lax.psum_scatter(part, 'xh', scatter_dimension=0, tiled=True)  33.4 us
    dot_general x1, matrix products, per_device(): ladder = jnp.dot(amps, integrals, preferred_element_type=jnp.float32)  30.5 us
    gather x3, local copies, waits for them, and re-layouts, per_device(): amps = gathered[pos_of_stored[inv[p_of_i]]]  25.3 us
    all_to_all x1, blocking collectives, per_device(): lax.all_to_all(stored, ROW_AXES, split_axis=1, concat_axis=0, tiled=True)  24 us
    gather x1, local copies, waits for them, and re-layouts, per_device(): difference = ladder - ladder[partner_i]  17.1 us
    sub x1, other arithmetic, per_device(): difference = ladder - ladder[partner_i]  14.4 us
  transfers between devices with their start and end apart: 3, of which 3 were waited for; matrix products, arithmetic and copies ran while one was open for 6% of the time, Pallas kernels for 0%

commit v1 on v0

--- a/solution.py
+++ b/solution.py
@@ -17,7 +17,10 @@
     total = local_rows * n_row * n_col
     block = total // n_row
     regrouped = lax.all_to_all(stored, ROW_AXES, split_axis=1, concat_axis=0, tiled=True)
-    gathered = lax.all_gather(regrouped, COL_AXES, axis=0, tiled=True)
+    devices = lax.axis_size(COL_AXES)
+    blocks = jnp.stack([regrouped for _ in range(devices)])
+    blocks = lax.all_to_all(blocks, COL_AXES, split_axis=0, concat_axis=0)
+    gathered = jnp.concatenate(blocks, axis=0)
     s = jnp.arange(total, dtype=jnp.int32)
     s_row = s // (local_rows * n_col)
     s_col = s // local_rows % n_col

time: 297 us -> 305 us (1.027)
  starting transfers between devices: 0.09 us -> 4.86 us
  local copies, waits for them, and re-layouts: 51.3 us -> 54.9 us
    all_to_all x0 -> x1, waiting for transfers between devices: none -> 55.9 us  [per_device(): blocks = lax.all_to_all(blocks, COL_AXES, split_axis=0, concat_axis=0)]
    all_gather x1 -> x0, waiting for transfers between devices: 53.2 us -> none  [per_device(): gathered = lax.all_gather(regrouped, COL_AXES, axis=0, tiled=True)]
    all_to_all x0 -> x1, starting transfers between devices: none -> 4.78 us  [per_device(): blocks = lax.all_to_all(blocks, COL_AXES, split_axis=0, concat_axis=0)]
    another operation x0 -> x1, local copies, waits for them, and re-layouts: none -> 3.52 us  [per_device(): blocks = jnp.stack([regrouped for _ in range(devices)])]
where the time goes in v1:
time: 305 us
  waiting for transfers between devices  160 us (52%)
  local copies, waits for them, and re-layouts  54.9 us (18%)
  matrix products  30.5 us (10%)
  blocking collectives  23.9 us (8%)
  other arithmetic  16.5 us (5%)
  between operations  13.5 us (4%)
  starting transfers between devices  4.86 us (2%)
    reduce_scatter x1, waiting for transfers between devices, per_device(): lax.psum_scatter(difference, ('z', 'core'), scatter_dimension=0, tiled=True)  71.1 us
    all_to_all x1, waiting for transfers between devices, per_device(): blocks = lax.all_to_all(blocks, COL_AXES, split_axis=0, concat_axis=0)  55.9 us
    reduce_scatter x1, waiting for transfers between devices, per_device(): part = lax.psum_scatter(part, 'xh', scatter_dimension=0, tiled=True)  33.3 us
    dot_general x1, matrix products, per_device(): ladder = jnp.dot(amps, integrals, preferred_element_type=jnp.float32)  30.5 us
    gather x3, local copies, waits for them, and re-layouts, per_device(): amps = gathered[pos_of_stored[inv[p_of_i]]]  25.3 us
    all_to_all x1, blocking collectives, per_device(): lax.all_to_all(stored, ROW_AXES, split_axis=1, concat_axis=0, tiled=True)  23.9 us
    gather x1, local copies, waits for them, and re-layouts, per_device(): difference = ladder - ladder[partner_i]  17.1 us
    sub x1, other arithmetic, per_device(): difference = ladder - ladder[partner_i]  14.4 us
  transfers between devices with their start and end apart: 3, of which 3 were waited for; matrix products, arithmetic and copies ran while one was open for 6% of the time, Pallas kernels for 0%

profile of v1, /device:TPU:1, one launch (start us, length us, event | category | flops | bytes accessed | tf_op | source)
XLA Modules:
  0.0 304.5 jit_solution(3793737830031540644)
XLA Ops:
  6.5 0.0 copy-start
  6.5 0.0 copy-start.2
  6.5 23.9 %all_to_all.21 = bf16[8,16,3200]{2,0,1:T(8,128)(2,1)S(1)} all-to-all(bf16[8,16,3200]{2,0,1:T(8,128)(2,1)} %bitcast.16), channel_id=1, replica_groups=mesh['z'=4,'xh'=2,'core'=2,'xl'=2,'y'=4] {'z','xh','core'}, dimensions={1} | all-to-all | bytes 1638400 | tf_op jit(solution)/shard_map/all_to_all | solution.py:19
  30.5 3.5 %stack.5 = bf16[8,128,3200]{2,1,0:T(8,128)(2,1)} broadcast(bf16[128,3200]{1,0:T(8,128)(2,1)S(1)} %bitcast.15), dimensions={1,2} | broadcast | bytes 7372800 | tf_op jit(solution)/shard_map/stack | solution.py:21
  34.0 4.8 %all-to-all-start.1 = ((bf16[8,128,3200]{2,1,0:T(8,128)(2,1)}), bf16[8,128,3200]{2,1,0:T(8,128)(2,1)}, u32[]{:S(2)}, u32[]{:S(2)}) async-start(bf16[8,128,3200]{2,1,0:T(8,128)(2,1)} %stack.5), calls=%async_computation.1 | async-start | bytes 13107200 | tf_op jit(solution)/shard_map/all_to_all | solution.py:22
  38.8 0.0 reduce-scatter.3.cloned.1.call-start
  38.9 0.0 copy-done
  38.9 4.5 %gather_fusion.3 = s32[1024]{0:T(1024)S(1)} fusion(s32[1024]{0:T(1024)S(1)} %copy-done, s32[1024]{0:T(1024)S(1)} %broadcast_clamp_fusion.1), kind=kCustom, calls=%fused_computation.3 | custom fusion | bytes 12288 | tf_op jit(solution)/shard_map/gather | solution.py:36
  43.4 0.0 copy-done.2
  43.5 4.3 %scatter_custom_fusion = s32[1024]{0:T(1024)S(1)} fusion(s32[1024]{0:T(1024)S(1)} %compare_select_fusion.8, s32[1024]{0:T(1024)S(1)} %iota.13, s32[]{:T(128)} %constant.129.clone.1), kind=kCustom, calls=%fused_computation.79 | custom fusion | bytes 4100 | tf_op jit(solution)/shard_map/scatter | solution.py:29
  47.8 4.5 %gather_fusion = s32[1024]{0:T(1024)S(1)} fusion(s32[1024]{0:T(1024)S(1)} %scatter_custom_fusion, s32[1024]{0:T(1024)S(1)} %broadcast_clamp_fusion.1), kind=kCustom, calls=%fused_computation | custom fusion | bytes 12288 | tf_op jit(solution)/shard_map/gather | solution.py:42
  52.3 4.5 %gather_fusion.1 = s32[1024]{0:T(1024)S(1)} fusion(s32[1024]{0:T(1024)S(1)} %get-tuple-element.5, s32[1024]{0:T(1024)S(1)} %get-tuple-element.6), kind=kCustom, calls=%fused_computation.1 | custom fusion | bytes 12288 | tf_op jit(solution)/shard_map/gather | solution.py:42
  56.9 0.1 compare_select_fusion
  57.0 55.9 %all-to-all-done.1 = bf16[8,128,3200]{2,1,0:T(8,128)(2,1)} async-done(((bf16[8,128,3200]{2,1,0:T(8,128)(2,1)}), bf16[8,128,3200]{2,1,0:T(8,128)(2,1)}, u32[]{:S(2)}, u32[]{:S(2)}) %all-to-all-start.1) | async-done | bytes 6553632 | tf_op jit(solution)/shard_map/all_to_all | solution.py:22
  112.9 16.3 %gather_fusion.2 = bf16[1024,3200]{1,0:T(8,128)(2,1)} fusion(bf16[1024,3200]{1,0:T(8,128)(2,1)} %bitcast.3, s32[1024]{0:T(1024)S(1)} %broadcast_clamp_fusion.3), kind=kCustom, calls=%fused_computation.2 | custom fusion | bytes 13111296 | tf_op jit(solution)/shard_map/gather | solution.py:42
  129.2 30.5 %fusion.24 = f32[1024,3200]{1,0:T(8,128)} fusion(bf16[1024,3200]{1,0:T(8,128)(2,1)} %gather_fusion.2, bf16[3200,3200]{1,0:T(8,128)(2,1)} %param.5), kind=kOutput, calls=%fused_computation.81 | convolution fusion | flops 20971520000 | bytes 40140800 | tf_op jit(solution)/shard_map/dot_general | solution.py:43
  159.7 17.1 %gather_fusion.4 = f32[1024,3200]{1,0:T(8,128)} fusion(f32[1024,3200]{1,0:T(8,128)} %fusion.24, s32[1024]{0:T(1024)S(1)} %broadcast_clamp_fusion), kind=kCustom, calls=%fused_computation.4 | custom fusion | bytes 26218496 | tf_op jit(solution)/shard_map/gather | solution.py:44
  176.8 0.0 copy-start.1
  176.9 14.4 %sub.51 = f32[1024,3200]{1,0:T(8,128)} subtract(f32[1024,3200]{1,0:T(8,128)} %fusion.24, f32[1024,3200]{1,0:T(8,128)} %gather_fusion.4) | non-fusion elementwise | flops 3276800 | bytes 39321600 | tf_op jit(solution)/shard_map/sub | solution.py:44
  191.2 0.0 reduce-scatter.3.cloned.1.call-update
  191.3 0.0 reduce-scatter.5.cloned.1.call-start
  191.3 71.1 %reduce-scatter.3.cloned.1.call-done = f32[128,3200]{1,0:T(8,128)} async-done(((f32[1024,3200]{1,0:T(8,128)}), f32[128,3200]{1,0:T(8,128)}) %reduce-scatter.3.cloned.1.call-update) | async-done | bytes 1638416 | tf_op jit(solution)/shard_map/reduce_scatter | solution.py:45
  262.4 0.0 reduce-scatter.5.cloned.1.call-update
  262.4 33.3 %reduce-scatter.5.cloned.1.call-done = f32[64,3200]{1,0:T(8,128)} async-done(((f32[128,3200]{1,0:T(8,128)}), f32[64,3200]{1,0:T(8,128)}) %reduce-scatter.5.cloned.1.call-update) | async-done | bytes 819216 | tf_op jit(solution)/shard_map/reduce_scatter | solution.py:46
  295.8 1.9 convert_element_type.3
  297.7 0.0 copy-done.1
  (9 shorter events, 0.1 us)
Async XLA Ops:
  6.5 32.4 %copy-start = (s32[1024]{0:T(1024)S(1)}, s32[1024]{0:T(1024)}, u32[]{:S(2)}) copy-start(s32[1024]{0:T(1024)} %param.7) | copy-start | bytes 12292
  6.5 36.9 %copy-start.2 = (s32[1024]{0:T(1024)S(1)}, s32[1024]{0:T(1024)}, u32[]{:S(2)}) copy-start(s32[1024]{0:T(1024)} %param.6) | copy-start | bytes 12292
  34.0 78.9 %all-to-all-start.1 = ((bf16[8,128,3200]{2,1,0:T(8,128)(2,1)}), bf16[8,128,3200]{2,1,0:T(8,128)(2,1)}, u32[]{:S(2)}, u32[]{:S(2)}) async-start(bf16[8,128,3200]{2,1,0:T(8,128)(2,1)} %stack.5), calls=%async_computation.1 | async-start | bytes 13107200 | tf_op jit(solution)/shard_map/all_to_all | solution.py:22
  38.8 223.6 %reduce-scatter.3.cloned.1.call-start = ((), (), s32[]{:S(2)}) async-start(), calls=%async_computation.4 | async-start | bytes 14745600 | tf_op jit(solution)/shard_map/reduce_scatter | solution.py:45
  176.8 120.8 %copy-start.1 = (s32[1024]{0:T(1024)S(1)}, s32[1024]{0:T(1024)}, u32[]{:S(2)}) copy-start(s32[1024]{0:T(1024)} %param.7) | copy-start | bytes 12292
  191.3 104.5 %reduce-scatter.5.cloned.1.call-start = ((), (), s32[]{:S(2)}) async-start(), calls=%async_computation.5 | async-start | bytes 2457600 | tf_op jit(solution)/shard_map/reduce_scatter | solution.py:46
Sparse Core Ops, SparseCore 0:
  191.4 70.9 reduce-scatter.2
  264.7 30.9 reduce-scatter.4
